TPU v7x, 256 devices: a whole 4x4x8 slice. The times are simulated.
256 devices in a mesh: gx: 8 (over y, core), gy: 32 (over x, z).
Axes of the slice: x: 4, y: 4, z: 8, core: 2. Of those that a mesh axis runs over, the one named last changes fastest.
Arguments:
- control: float32 [1, 2, 6, 1536, 3072], P(None, None, None, 'gy', 'gx'), may hold values from -6 to 6
- sigma: float32 [2, 6, 1536, 3072], P(None, None, 'gy', 'gx'), may hold values from 0.5 to 5
- kappa: float32 [5, 1536, 3072], P(None, 'gy', 'gx'), may hold values from 0.05 to 5
- beta: float32 [6, 1536, 3072], P(None, 'gy', 'gx'), may hold values from -3 to 3
- sea_mask: int32 [1536, 3072], P('gy', 'gx'), may hold values 0 or 1
- x_inverse: float32 [3072, 3072], P('gx'), as said below
- y_inverse: float32 [1536, 1536], P('gx')
- ssh_coef: float32 [2, 6], replicated, may hold values from -1.5 to 1.5
- obs_owner: int32 [65536, 1], P(('gx', 'gy')), may hold values from 0 to 255; in each aligned block of 256 rows (0 to 255, 256 to 511, ...) at most 2 rows name the same one
- tile_index: int32 [65536], P(('gx', 'gy')), may hold values from 0 to 18046, as said below
- obs_frac: float32 [2, 65536], P(None, ('gx', 'gy')), may hold values from 0 to 1
- obs_count: int32 [256], P(('gx', 'gy')), may hold values from 128 to 256
Outputs:
- increments: float32 [1, 2, 6, 1536, 3072], P(None, None, None, 'gy', 'gx')
- sea_height: float32 [1, 1536, 3072], P(None, 'gy', 'gx')
- obs_equiv: float32 [2, 13, 65536], P(None, None, ('gx', 'gy'))
Inputs may be any that keep to these rules, and one draw needn't show every extreme that they name: `obs_owner`: among the slots of one device, at most 2 name the same owner. `tile_index`: row * 384 + column of a cell in the device's own tile, with row below 47 and column below 383. `x_inverse`: the zonal inverse is symmetric.
All inputs are finite; a program needn't handle non-finite values. No bound on the sum of `sea_mask` on one device may be relied on, other than what follows from the above.
Results may differ from a plain program's by a relative error of at most 0.00013.
Values sent between devices are 32-bit elements; how exact they have to be, the bound alone decides.
A program may use at most 128 MiB of HBM per device.

v0:
```python
import jax
import jax.numpy as jnp
from jax import lax
from jax.sharding import PartitionSpec as P

STEPS = 2
CAP = 2


def vertical(values, kappa):
    levels = values.shape[2]
    c_list = []
    d_list = []
    for level in range(levels):
        k_below = kappa[level - 1] if level > 0 else 0.0
        k_above = kappa[level] if level < levels - 1 else 0.0
        diag_term = 1.0 + k_below + k_above
        if level == 0:
            pivot = diag_term
            d_new = values[:, :, 0] / pivot
        else:
            pivot = diag_term + k_below * c_list[-1]
            d_new = (values[:, :, level] + k_below * d_list[-1]) / pivot
        c_list.append(-k_above / pivot)
        d_list.append(d_new)
    result = [d_list[-1]]
    for level in range(levels - 2, -1, -1):
        result.insert(0, d_list[level] - c_list[level] * result[0])
    return jnp.stack(result, axis=2)


def body(
    control,
    sigma,
    kappa,
    beta,
    sea_mask,
    x_inverse,
    y_inverse,
    ssh_coef,
    obs_owner,
    tile_index,
    obs_frac,
    obs_count,
):
    highest = lax.Precision.HIGHEST
    vec_count, kinds, levels, lat_rows, lon_cols = control.shape
    field_count = vec_count * kinds * levels
    sea_open = sea_mask.astype(jnp.float32)
    grid_field = control.reshape(field_count, lat_rows, lon_cols)
    whole_y = lax.all_gather(y_inverse, "gx", axis=0, tiled=True)
    for diffusion_step in range(STEPS):
        grid_field = sea_open * jnp.einsum(
            "fyb,ab->fya",
            lax.all_gather(grid_field, "gx", axis=2, tiled=True),
            x_inverse,
            precision=highest,
        )
        turned = jnp.swapaxes(grid_field, 1, 2)
        merid_lines = lax.all_to_all(turned, "gy", split_axis=1, concat_axis=2, tiled=True)
        solved = jnp.einsum("fxb,ab->fxa", merid_lines, whole_y, precision=highest)
        returned = lax.all_to_all(solved, "gy", split_axis=2, concat_axis=1, tiled=True)
        grid_field = sea_open * jnp.swapaxes(returned, 1, 2)
        grid_field = vertical(
            grid_field.reshape(vec_count, kinds, levels, lat_rows, lon_cols), kappa
        ).reshape(field_count, lat_rows, lon_cols)
    grid_field = grid_field.reshape(vec_count, kinds, levels, lat_rows, lon_cols)
    temper = sigma[0] * grid_field[:, 0]
    saline = sigma[1] * grid_field[:, 1] + beta * temper
    height = jnp.sum(
        ssh_coef[0][None, :, None, None] * temper + ssh_coef[1][None, :, None, None] * saline,
        axis=1,
    )
    increments = jnp.stack([temper, saline], axis=1)
    profile = jnp.concatenate([temper, saline, height[:, None]], axis=1)
    slot_total = tile_index.shape[0]
    row_index = tile_index // lon_cols
    col_index = tile_index % lon_cols
    frac_x = obs_frac[0]
    frac_y = obs_frac[1]
    corner_a = profile[:, :, row_index, col_index]
    corner_b = profile[:, :, row_index, col_index + 1]
    corner_c = profile[:, :, row_index + 1, col_index]
    corner_d = profile[:, :, row_index + 1, col_index + 1]
    interp = (1.0 - frac_y) * ((1.0 - frac_x) * corner_a + frac_x * corner_b) + frac_y * (
        (1.0 - frac_x) * corner_c + frac_x * corner_d
    )
    live_slot = (jnp.arange(slot_total, dtype=jnp.int32) < obs_count[0]).astype(jnp.float32)
    record_len = interp.shape[0] * interp.shape[1]
    interp = (interp * live_slot).reshape(record_len, slot_total)
    gx_count = lax.axis_size("gx")
    gy_count = lax.axis_size("gy")
    device_total = gx_count * gy_count
    owners = obs_owner[:, 0]
    one_hot = (owners[:, None] == jnp.arange(device_total, dtype=jnp.int32)[None, :]).astype(
        jnp.int32
    )
    before = jnp.cumsum(one_hot, axis=0) - one_hot
    slot_rank = jnp.sum(before * one_hot, axis=1)
    outgoing = (
        jnp.zeros((CAP, record_len, device_total), jnp.float32)
        .at[slot_rank, :, owners]
        .set(interp.T)
    )
    outgoing = outgoing.reshape(CAP, record_len, gx_count, gy_count)
    arrived = lax.all_to_all(
        lax.all_to_all(outgoing, "gx", split_axis=2, concat_axis=2, tiled=True),
        "gy",
        split_axis=3,
        concat_axis=3,
        tiled=True,
    )
    obs_equiv = arrived.reshape(CAP, record_len, device_total)
    return (increments, height, obs_equiv)


def solution(mesh):
    return jax.shard_map(
        body,
        mesh=mesh,
        in_specs=(
            P(None, None, None, "gy", "gx"),
            P(None, None, "gy", "gx"),
            P(None, "gy", "gx"),
            P(None, "gy", "gx"),
            P("gy", "gx"),
            P("gx", None),
            P("gx", None),
            P(),
            P(("gx", "gy"), None),
            P(("gx", "gy")),
            P(None, ("gx", "gy")),
            P(("gx", "gy")),
        ),
        out_specs=(
            P(None, None, None, "gy", "gx"),
            P(None, "gy", "gx"),
            P(None, None, ("gx", "gy")),
        ),
        check_vma=False,
    )
```

profile of v0, /device:TPU:1, one launch (start us, length us, event | category | flops | bytes accessed | tf_op | source)
XLA Modules:
  0.0 489.2 jit_solution(15231277766906948029)
XLA Ops:
  9.6 51.3 %all-gather.4.cloned.1.call-done = f32[12,48,3072]{2,1,0:T(8,128)} async-done(((f32[12,48,384]{2,1,0:T(8,128)}), f32[12,48,3072]{2,1,0:T(8,128)}) %all-gather.4.cloned.1.call-update) | async-done | bytes 7077904 | tf_op jit(solution)/shard_map/all_gather | solution.py:55
  60.9 15.1 %fusion.11 = f32[12,384,48]{1,2,0:T(8,128)} fusion(f32[12,48,3072]{2,1,0:T(8,128)} %all-gather.4.cloned.1.call-done, f32[384,3072]{1,0:T(8,128)} %param.17, f32[384,48]{0,1:T(8,128)S(1)} %get-tuple-element.41), kind=kOutput, calls=%fused_computation.16 | convolution fusion | flops 8153948160 | bytes 12754944 | tf_op jit(solution)/shard_map/fyb,ab->fya/dot_general | solution.py:53
  78.4 3.3 reshape.729
  81.7 42.5 %all_to_all.82 = f32[32,1,6912]{2,1,0:T(1,128)S(1)} all-to-all(f32[32,1,6912]{2,1,0:T(1,128)} %reshape.729), channel_id=1, replica_groups=mesh['gx'=8,'gy'=32] {'gy'}, dimensions={0} | all-to-all | bytes 1769472 | tf_op jit(solution)/shard_map/all_to_all | solution.py:60
  124.7 3.8 reduce.1
  134.2 3.1 all_to_all.61
  137.4 12.0 %fusion.2 = f32[12,12,1536]{2,1,0:T(8,128)S(1)} fusion(f32[12,12,1536]{2,1,0:T(8,128)S(1)} %all_to_all.61, f32[1536,1536]{1,0:T(8,128)} %all-gather.6.cloned.1.call-done), kind=kOutput, calls=%fused_computation.7 | convolution fusion | flops 4076863488 | bytes 11206656 | tf_op jit(solution)/shard_map/fxb,ab->fxa/dot_general | solution.py:61
  149.4 8.6 %copy.95 = f32[12,12,1536]{1,0,2:T(8,128)} copy(f32[12,12,1536]{2,1,0:T(8,128)S(1)} %fusion.2) | data formatting | bytes 1769472 | tf_op jit(solution)/shard_map/fxb,ab->fxa/dot_general | solution.py:61
  158.0 10.0 %reshape.731 = f32[32,1,6912]{2,1,0:T(1,128)} reshape(f32[1536,12,12]{2,1,0:T(8,128)} %bitcast.172) | data formatting | bytes 1769472
  168.0 8.0 %all-to-all-start.1 = ((f32[32,1,6912]{2,1,0:T(1,128)}), f32[32,1,6912]{2,1,0:T(1,128)S(1)}, u32[]{:S(2)}, u32[]{:S(2)}) async-start(f32[32,1,6912]{2,1,0:T(1,128)} %reshape.731), calls=%async_computation.1 | async-start | bytes 1769472 | tf_op jit(solution)/shard_map/all_to_all | solution.py:62
  180.4 17.1 %all-to-all-done.1 = f32[32,1,6912]{2,1,0:T(1,128)S(1)} async-done(((f32[32,1,6912]{2,1,0:T(1,128)}), f32[32,1,6912]{2,1,0:T(1,128)S(1)}, u32[]{:S(2)}, u32[]{:S(2)}) %all-to-all-start.1) | async-done | bytes 884768 | tf_op jit(solution)/shard_map/all_to_all | solution.py:62
  200.2 8.0 %reshape.732 = f32[1536,12,12]{2,1,0:T(8,128)} reshape(f32[32,6912]{1,0:T(8,128)S(1)} %reduce.2) | data formatting | bytes 1769472
  208.2 9.7 %copy.96 = f32[12,12,32,48]{3,1,2,0:T(8,128)S(1)} copy(f32[12,12,32,48]{1,0,3,2:T(8,128)} %bitcast.174) | data formatting | bytes 1769472 | tf_op jit(solution)/shard_map/all_to_all | solution.py:62
  225.6 46.7 %all-gather.8.cloned.1.call-done = f32[12,48,3072]{2,1,0:T(8,128)} async-done(((f32[12,48,384]{2,1,0:T(8,128)}), f32[12,48,3072]{2,1,0:T(8,128)}) %all-gather.8.cloned.1.call-update) | async-done | bytes 7077904 | tf_op jit(solution)/shard_map/all_gather | solution.py:55
  272.4 15.1 %fusion.17 = f32[12,384,48]{1,2,0:T(8,128)} fusion(f32[12,48,3072]{2,1,0:T(8,128)} %all-gather.8.cloned.1.call-done, f32[384,3072]{1,0:T(8,128)} %param.17, f32[384,48]{0,1:T(8,128)S(1)} %copy-done.8), kind=kOutput, calls=%fused_computation.18 | convolution fusion | flops 8153948160 | bytes 12754944 | tf_op jit(solution)/shard_map/fyb,ab->fya/dot_general | solution.py:53
  289.8 3.3 reshape.733
  293.1 9.7 %all-to-all-start.2 = ((f32[32,1,6912]{2,1,0:T(1,128)}), f32[32,1,6912]{2,1,0:T(1,128)S(1)}, u32[]{:S(2)}, u32[]{:S(2)}) async-start(f32[32,1,6912]{2,1,0:T(1,128)} %reshape.733), calls=%async_computation.2 | async-start | bytes 1769472 | tf_op jit(solution)/shard_map/all_to_all | solution.py:60
  303.9 20.3 %all-to-all-done.2 = f32[32,1,6912]{2,1,0:T(1,128)S(1)} async-done(((f32[32,1,6912]{2,1,0:T(1,128)}), f32[32,1,6912]{2,1,0:T(1,128)S(1)}, u32[]{:S(2)}, u32[]{:S(2)}) %all-to-all-start.2) | async-done | bytes 884768 | tf_op jit(solution)/shard_map/all_to_all | solution.py:60
  324.2 3.8 reduce.3
  333.7 3.1 all_to_all.69
  336.8 12.0 %fusion = f32[12,12,1536]{2,1,0:T(8,128)S(1)} fusion(f32[12,12,1536]{2,1,0:T(8,128)S(1)} %all_to_all.69, f32[1536,1536]{1,0:T(8,128)} %all-gather.6.cloned.1.call-done), kind=kOutput, calls=%fused_computation.5 | convolution fusion | flops 4076863488 | bytes 11206656 | tf_op jit(solution)/shard_map/fxb,ab->fxa/dot_general | solution.py:61
  348.8 8.8 %copy.101 = f32[12,12,1536]{1,0,2:T(8,128)} copy(f32[12,12,1536]{2,1,0:T(8,128)S(1)} %fusion) | data formatting | bytes 1769472 | tf_op jit(solution)/shard_map/fxb,ab->fxa/dot_general | solution.py:61
  357.7 10.0 %reshape.735 = f32[32,1,6912]{2,1,0:T(1,128)} reshape(f32[1536,12,12]{2,1,0:T(8,128)} %bitcast.173) | data formatting | bytes 1769472
  367.7 8.4 %all-to-all-start.3 = ((f32[32,1,6912]{2,1,0:T(1,128)}), f32[32,1,6912]{2,1,0:T(1,128)S(1)}, u32[]{:S(2)}, u32[]{:S(2)}) async-start(f32[32,1,6912]{2,1,0:T(1,128)} %reshape.735), calls=%async_computation.3 | async-start | bytes 1769472 | tf_op jit(solution)/shard_map/all_to_all | solution.py:62
  376.5 21.0 %all-to-all-done.3 = f32[32,1,6912]{2,1,0:T(1,128)S(1)} async-done(((f32[32,1,6912]{2,1,0:T(1,128)}), f32[32,1,6912]{2,1,0:T(1,128)S(1)}, u32[]{:S(2)}, u32[]{:S(2)}) %all-to-all-start.3) | async-done | bytes 884768 | tf_op jit(solution)/shard_map/all_to_all | solution.py:62
  400.3 7.6 %reshape.736 = f32[1536,12,12]{2,1,0:T(8,128)} reshape(f32[32,6912]{1,0:T(8,128)S(1)} %reduce.4) | data formatting | bytes 1769472
  407.9 9.7 %copy.102 = f32[12,12,32,48]{3,1,2,0:T(8,128)S(1)} copy(f32[12,12,32,48]{1,0,3,2:T(8,128)} %bitcast.175) | data formatting | bytes 1769472 | tf_op jit(solution)/shard_map/all_to_all | solution.py:62
  424.9 5.7 %copy.106 = f32[1,13,48,384]{1,3,2,0:T(8,128)} copy(f32[1,13,48,384]{3,2,1,0:T(8,128)S(1)} %pad_maximum_fusion) | data formatting | bytes 1916928 | tf_op jit(solution)/shard_map/concatenate | solution.py:75
  440.4 12.1 %scatter_fusion = f32[2,13,256]{1,2,0:T(8,128)S(1)} fusion(f32[2,13,256]{1,2,0:T(8,128)S(1)} %broadcast_in_dim.15, s32[256]{0:T(256)S(1)} %bitcast.176, f32[256,13]{1,0:T(8,128)S(1)} %copy.111), kind=kCustom, calls=%fused_computation.4 | custom fusion | bytes 41984 | tf_op jit(solution)/shard_map/scatter | solution.py:103
  452.8 12.6 %all_to_all.83 = f32[8,1,832]{2,1,0:T(1,128)S(1)} all-to-all(f32[8,1,832]{2,1,0:T(1,128)S(1)} %reshape.737), channel_id=1, replica_groups=mesh['gx'=8,'gy'=32] {'gx'}, dimensions={0} | all-to-all | bytes 53248 | tf_op jit(solution)/shard_map/all_to_all | solution.py:107
  467.2 4.5 all-to-all-start.5
  472.7 7.8 %all-to-all-done.5 = f32[32,1,208]{2,1,0:T(1,128)S(1)} async-done(((f32[32,1,208]{2,1,0:T(1,128)}), f32[32,1,208]{2,1,0:T(1,128)S(1)}, u32[]{:S(2)}, u32[]{:S(2)}) %all-to-all-start.5) | async-done | bytes 26656 | tf_op jit(solution)/shard_map/all_to_all | solution.py:106
  (113 shorter events, 59.1 us)
Async XLA Ops:
  7.2 53.7 %all-gather.4.cloned.1.call-start = ((), (), s32[]{:S(2)}) async-start(), calls=%async_computation.6 | async-start | bytes 7962624 | tf_op jit(solution)/shard_map/all_gather | solution.py:55
  7.9 129.5 %all-gather.6.cloned.1.call-start = ((), (), s32[]{:S(2)}) async-start(), calls=%async_computation.7 | async-start | bytes 10616832 | tf_op jit(solution)/shard_map/all_gather | solution.py:51
  9.5 51.3 %copy-start.7 = (f32[384,48]{0,1:T(8,128)}, f32[384,48]{0,1:T(8,128)S(1)}, u32[]{:S(2)}) copy-start(f32[384,48]{0,1:T(8,128)S(1)} %get-tuple-element.41) | copy-start | bytes 221188
  158.0 18.9 %copy-start = (f32[5,48,384]{2,1,0:T(8,128)S(1)}, f32[5,48,384]{2,1,0:T(8,128)}, u32[]{:S(2)}) copy-start(f32[5,48,384]{2,1,0:T(8,128)} %param.14) | copy-start | bytes 1105924
  168.0 29.5 %all-to-all-start.1 = ((f32[32,1,6912]{2,1,0:T(1,128)}), f32[32,1,6912]{2,1,0:T(1,128)S(1)}, u32[]{:S(2)}, u32[]{:S(2)}) async-start(f32[32,1,6912]{2,1,0:T(1,128)} %reshape.731), calls=%async_computation.1 | async-start | bytes 1769472 | tf_op jit(solution)/shard_map/all_to_all | solution.py:62
  176.0 96.3 %all-gather.8.cloned.1.call-start = ((), (), s32[]{:S(2)}) async-start(), calls=%async_computation.8 | async-start | bytes 7962624 | tf_op jit(solution)/shard_map/all_gather | solution.py:55
  177.6 2.8 copy-start.3
  178.3 0.6 copy-start.2
  222.2 50.2 %copy-start.8 = (f32[384,48]{0,1:T(8,128)S(1)}, f32[384,48]{0,1:T(8,128)}, u32[]{:S(2)}) copy-start(f32[384,48]{0,1:T(8,128)} %copy-done.7) | copy-start | bytes 221188
  224.7 0.9 copy-start.1
  287.5 16.0 %copy-start.11 = (s32[256,1]{0,1:T(1,128)S(1)}, s32[256,1]{0,1:T(1,128)}, u32[]{:S(2)}) copy-start(s32[256,1]{0,1:T(1,128)} %param.20) | copy-start | bytes 3076
  293.1 31.1 %all-to-all-start.2 = ((f32[32,1,6912]{2,1,0:T(1,128)}), f32[32,1,6912]{2,1,0:T(1,128)S(1)}, u32[]{:S(2)}, u32[]{:S(2)}) async-start(f32[32,1,6912]{2,1,0:T(1,128)} %reshape.733), calls=%async_computation.2 | async-start | bytes 1769472 | tf_op jit(solution)/shard_map/all_to_all | solution.py:60
  303.8 20.4 %copy-start.4 = (s32[256,2,128]{0,1,2:T(2,128)}, s32[256,2,128]{0,1,2:T(2,128)S(1)}, u32[]{:S(2)}) copy-start(s32[256,2,128]{0,1,2:T(2,128)S(1)} %fusion.23) | copy-start | bytes 786436
  303.9 29.8 %copy-start.12 = (s32[256,3]{0,1:T(4,128)}, s32[256,3]{0,1:T(4,128)S(1)}, u32[]{:S(2)}) copy-start(s32[256,3]{0,1:T(4,128)S(1)} %reduce-window.9) | copy-start | bytes 9220
  357.7 18.4 %slice-start = ((s32[256,3]{0,1:T(4,128)}), s32[256,2]{0,1:T(2,128)S(1)}, s32[]{:S(2)}) async-start(s32[256,3]{0,1:T(4,128)} %copy-done.12), calls=%async_computation.9 | async-start | bytes 4096 | tf_op jit(solution)/shard_map/slice.1
  357.7 18.4 %copy-start.5 = (s32[256,2,128]{0,1,2:T(2,128)S(1)}, s32[256,2,128]{0,1,2:T(2,128)}, u32[]{:S(2)}) copy-start(s32[256,2,128]{0,1,2:T(2,128)} %copy-done.4) | copy-start | bytes 786436
  357.7 18.7 %copy-start.15 = (f32[2,6]{1,0:T(2,128)S(1)}, f32[2,6]{1,0:T(2,128)}, u32[]{:S(2)}) copy-start(f32[2,6]{1,0:T(2,128)} %param.19) | copy-start | bytes 148
  357.7 18.7 %copy-start.13 = (s32[256]{0:T(256)S(1)}, s32[256]{0:T(256)}, u32[]{:S(2)}) copy-start(s32[256]{0:T(256)} %param.21) | copy-start | bytes 3076
  357.7 18.7 %copy-start.14 = (f32[2,256]{1,0:T(2,128)S(1)}, f32[2,256]{1,0:T(2,128)}, u32[]{:S(2)}) copy-start(f32[2,256]{1,0:T(2,128)} %param.22) | copy-start | bytes 6148
  367.7 29.8 %all-to-all-start.3 = ((f32[32,1,6912]{2,1,0:T(1,128)}), f32[32,1,6912]{2,1,0:T(1,128)S(1)}, u32[]{:S(2)}, u32[]{:S(2)}) async-start(f32[32,1,6912]{2,1,0:T(1,128)} %reshape.735), calls=%async_computation.3 | async-start | bytes 1769472 | tf_op jit(solution)/shard_map/all_to_all | solution.py:62
  421.9 2.6 copy-start.6
  421.9 2.6 copy-start.9
  424.8 5.8 %copy-start.10 = (f32[48,384]{1,0:T(8,128)}, f32[48,384]{1,0:T(8,128)S(1)}, u32[]{:S(2)}) copy-start(f32[48,384]{1,0:T(8,128)S(1)} %get-tuple-element.11) | copy-start | bytes 221188
  467.2 13.2 %all-to-all-start.5 = ((f32[32,1,208]{2,1,0:T(1,128)}), f32[32,1,208]{2,1,0:T(1,128)S(1)}, u32[]{:S(2)}, u32[]{:S(2)}) async-start(f32[32,1,208]{2,1,0:T(1,128)} %reshape.739), calls=%async_computation.5 | async-start | bytes 65536 | tf_op jit(solution)/shard_map/all_to_all | solution.py:106
Sparse Core Ops, SparseCore 0:
  9.8 51.0 all-gather.3
  62.7 56.8 all-gather.5
  225.8 46.5 all-gather.7
where the time goes:
time: 498 us; the launch traced here: 489 us
  waiting for transfers between devices  166 us (33%)
  local copies, waits for them, and re-layouts  140 us (28%)
  blocking collectives  55.1 us (11%)
  matrix products  54.3 us (11%)
  starting transfers between devices  30.7 us (6%)
  other arithmetic  28 us (6%)
  between operations  15.3 us (3%)
    all_gather x2, waiting for transfers between devices, body(): lax.all_gather(grid_field, 'gx', axis=2, tiled=True)  98 us
    unnamed x49, local copies, waits for them, and re-layouts  50.9 us
    all_to_all x1, blocking collectives, body(): lax.all_to_all(turned, 'gy', split_axis=1, concat_axis=2, tiled=True)  42.5 us
    all_to_all x2, waiting for transfers between devices, body(): lax.all_to_all(solved, 'gy', split_axis=2, concat_axis=1, tiled=True)  38.1 us
    dot_general x2, matrix products, body(): jnp.einsum('fyb,ab->fya', lax.all_gather(grid_field, 'gx', axis=2, tiled=...  30.3 us
    dot_general x2, matrix products, body(): solved = jnp.einsum('fxb,ab->fxa', merid_lines, whole_y, precision=highest)  24 us
    all_to_all x4, local copies, waits for them, and re-layouts, body(): lax.all_to_all(solved, 'gy', split_axis=2, concat_axis=1, tiled=True)  22.5 us
    all_to_all x1, waiting for transfers between devices, body(): lax.all_to_all(turned, 'gy', split_axis=1, concat_axis=2, tiled=True)  20.3 us
  transfers between devices with their start and end apart: 7, of which 6 were waited for; matrix products, arithmetic and copies ran while one was open for 8% of the time, Pallas kernels for 0%

commit v1 on v0

--- a/solution.py
+++ b/solution.py
@@ -52,7 +52,9 @@
     for diffusion_step in range(STEPS):
         grid_field = sea_open * jnp.einsum(
             "fyb,ab->fya",
-            lax.all_gather(grid_field, "gx", axis=2, tiled=True),
+            jnp.concatenate(
+                lax.all_to_all(jnp.stack([grid_field] * lax.axis_size("gx")), "gx", 0, 0), axis=2
+            ),
             x_inverse,
             precision=highest,
         )

time: 498 us -> 603 us (1.21)
  blocking collectives: 55.1 us -> 132 us
  waiting for transfers between devices: 166 us -> 185 us
  local copies, waits for them, and re-layouts: 140 us -> 149 us
    all_to_all x0 -> x1, waiting for transfers between devices: none -> 118 us  [body(): lax.all_to_all(jnp.stack([grid_field] * lax.axis_size('gx')), 'gx', 0, 0)]
    all_gather x2 -> x0, waiting for transfers between devices: 98 us -> none  [body(): lax.all_gather(grid_field, 'gx', axis=2, tiled=True)]
    all_to_all x0 -> x1, blocking collectives: none -> 88.6 us  [body(): lax.all_to_all(jnp.stack([grid_field] * lax.axis_size('gx')), 'gx', 0, 0)]
    all_to_all x1, blocking collectives: 42.5 us -> 31 us  [body(): lax.all_to_all(turned, 'gy', split_axis=1, concat_axis=2, tiled=True)]
    all_to_all x0 -> x1, starting transfers between devices: none -> 8.07 us  [body(): lax.all_to_all(jnp.stack([grid_field] * lax.axis_size('gx')), 'gx', 0, 0)]
    unnamed x49 -> x53, local copies, waits for them, and re-layouts: 50.9 us -> 49.9 us
  transfers between devices with their start and end apart: 7 -> 6, of which waited for: 6 -> 5; matrix products, arithmetic and copies ran while one was open for 8% -> 7% of each run, Pallas kernels for 0% -> 0%
where the time goes in v1:
time: 603 us; the launch traced here: 593 us
  waiting for transfers between devices  185 us (31%)
  local copies, waits for them, and re-layouts  149 us (25%)
  blocking collectives  132 us (22%)
  matrix products  50.5 us (8%)
  starting transfers between devices  34.5 us (6%)
  other arithmetic  27.1 us (4%)
  between operations  15.4 us (3%)
    all_to_all x1, waiting for transfers between devices, body(): lax.all_to_all(jnp.stack([grid_field] * lax.axis_size('gx')), 'gx', 0, 0)  118 us
    all_to_all x1, blocking collectives, body(): lax.all_to_all(jnp.stack([grid_field] * lax.axis_size('gx')), 'gx', 0, 0)  88.6 us
    unnamed x53, local copies, waits for them, and re-layouts  49.9 us
    all_to_all x2, waiting for transfers between devices, body(): lax.all_to_all(solved, 'gy', split_axis=2, concat_axis=1, tiled=True)  38.2 us
    all_to_all x1, blocking collectives, body(): lax.all_to_all(turned, 'gy', split_axis=1, concat_axis=2, tiled=True)  31 us
    dot_general x2, matrix products, body(): jnp.einsum('fyb,ab->fya', jnp.concatenate(lax.all_to_all(jnp.stack([grid_...  26.6 us
    dot_general x2, matrix products, body(): solved = jnp.einsum('fxb,ab->fxa', merid_lines, whole_y, precision=highest)  24 us
    all_to_all x4, local copies, waits for them, and re-layouts, body(): lax.all_to_all(solved, 'gy', split_axis=2, concat_axis=1, tiled=True)  22.5 us
  transfers between devices with their start and end apart: 6, of which 5 were waited for; matrix products, arithmetic and copies ran while one was open for 7% of the time, Pallas kernels for 0%

profile of v1, /device:TPU:1, one launch (start us, length us, event | category | flops | bytes accessed | tf_op | source)
XLA Modules:
  0.0 593.3 jit_solution(5878513302031680493)
XLA Ops:
  7.9 4.6 stack.14
  12.5 8.1 %all-to-all-start = ((f32[8,12,48,384]{3,2,1,0:T(8,128)}), f32[8,12,48,384]{3,2,1,0:T(8,128)}, u32[]{:S(2)}, u32[]{:S(2)}) async-start(f32[8,12,48,384]{3,2,1,0:T(8,128)} %stack.14), calls=%async_computation | async-start | bytes 14155776 | tf_op jit(solution)/shard_map/all_to_all | solution.py:56
  20.6 117.7 %all-to-all-done = f32[8,12,48,384]{3,2,1,0:T(8,128)} async-done(((f32[8,12,48,384]{3,2,1,0:T(8,128)}), f32[8,12,48,384]{3,2,1,0:T(8,128)}, u32[]{:S(2)}, u32[]{:S(2)}) %all-to-all-start) | async-done | bytes 7077920 | tf_op jit(solution)/shard_map/all_to_all | solution.py:56
  138.3 4.0 copy.124
  142.3 14.1 %fusion.11 = f32[12,384,48]{1,2,0:T(8,128)} fusion(f32[12,48,3072]{2,1,0:T(8,128)S(1)} %bitcast.184, f32[384,3072]{1,0:T(8,128)} %param.17, f32[384,48]{0,1:T(8,128)S(1)} %get-tuple-element.41), kind=kOutput, calls=%fused_computation.16 | convolution fusion | flops 8153948160 | bytes 12754944 | tf_op jit(solution)/shard_map/fyb,ab->fya/dot_general | solution.py:53
  162.1 31.0 %all_to_all.92 = f32[32,1,6912]{2,1,0:T(1,128)S(1)} all-to-all(f32[32,1,6912]{2,1,0:T(1,128)} %reshape.741), channel_id=1, replica_groups=mesh['gx'=8,'gy'=32] {'gy'}, dimensions={0} | all-to-all | bytes 1769472 | tf_op jit(solution)/shard_map/all_to_all | solution.py:62
  193.6 3.8 reduce.1
  206.3 12.0 %fusion.2 = f32[12,12,1536]{2,1,0:T(8,128)S(1)} fusion(f32[12,12,1536]{2,1,0:T(8,128)S(1)} %all_to_all.68, f32[1536,1536]{1,0:T(8,128)} %all-gather.2.cloned.1.call-done), kind=kOutput, calls=%fused_computation.7 | convolution fusion | flops 4076863488 | bytes 11206656 | tf_op jit(solution)/shard_map/fxb,ab->fxa/dot_general | solution.py:63
  218.3 8.7 %copy.99 = f32[12,12,1536]{1,0,2:T(8,128)} copy(f32[12,12,1536]{2,1,0:T(8,128)S(1)} %fusion.2) | data formatting | bytes 1769472 | tf_op jit(solution)/shard_map/fxb,ab->fxa/dot_general | solution.py:63
  226.9 10.1 %reshape.743 = f32[32,1,6912]{2,1,0:T(1,128)} reshape(f32[1536,12,12]{2,1,0:T(8,128)} %bitcast.178) | data formatting | bytes 1769472
  237.0 8.4 %all-to-all-start.2 = ((f32[32,1,6912]{2,1,0:T(1,128)}), f32[32,1,6912]{2,1,0:T(1,128)S(1)}, u32[]{:S(2)}, u32[]{:S(2)}) async-start(f32[32,1,6912]{2,1,0:T(1,128)} %reshape.743), calls=%async_computation.2 | async-start | bytes 1769472 | tf_op jit(solution)/shard_map/all_to_all | solution.py:64
  249.7 17.2 %all-to-all-done.2 = f32[32,1,6912]{2,1,0:T(1,128)S(1)} async-done(((f32[32,1,6912]{2,1,0:T(1,128)}), f32[32,1,6912]{2,1,0:T(1,128)S(1)}, u32[]{:S(2)}, u32[]{:S(2)}) %all-to-all-start.2) | async-done | bytes 884768 | tf_op jit(solution)/shard_map/all_to_all | solution.py:64
  269.7 7.7 %reshape.744 = f32[1536,12,12]{2,1,0:T(8,128)} reshape(f32[32,6912]{1,0:T(8,128)S(1)} %reduce.2) | data formatting | bytes 1769472
  277.4 9.7 %copy.100 = f32[12,12,32,48]{3,1,2,0:T(8,128)S(1)} copy(f32[12,12,32,48]{1,0,3,2:T(8,128)} %bitcast.180) | data formatting | bytes 1769472 | tf_op jit(solution)/shard_map/all_to_all | solution.py:64
  294.5 88.6 %all_to_all.93 = f32[8,12,48,384]{3,2,1,0:T(8,128)S(1)} all-to-all(f32[8,12,48,384]{3,2,1,0:T(8,128)S(1)} %stack.16), channel_id=1, replica_groups=mesh['gx'=8,'gy'=32] {'gx'}, dimensions={0} | all-to-all | bytes 14155776 | tf_op jit(solution)/shard_map/all_to_all | solution.py:56
  384.2 12.4 %fusion.17 = f32[12,384,48]{1,2,0:T(8,128)} fusion(f32[12,48,3072]{2,1,0:T(8,128)S(1)} %bitcast.183, f32[384,3072]{1,0:T(8,128)S(1)} %bitcast.186, f32[384,48]{0,1:T(8,128)S(1)} %copy-done.7), kind=kOutput, calls=%fused_computation.18 | convolution fusion | flops 8153948160 | bytes 12754944 | tf_op jit(solution)/shard_map/fyb,ab->fya/dot_general | solution.py:53
  399.0 3.3 reshape.745
  402.3 4.9 all-to-all-start.4
  408.2 20.3 %all-to-all-done.4 = f32[32,1,6912]{2,1,0:T(1,128)S(1)} async-done(((f32[32,1,6912]{2,1,0:T(1,128)}), f32[32,1,6912]{2,1,0:T(1,128)S(1)}, u32[]{:S(2)}, u32[]{:S(2)}) %all-to-all-start.4) | async-done | bytes 884768 | tf_op jit(solution)/shard_map/all_to_all | solution.py:62
  428.6 3.8 reduce.3
  441.2 12.0 %fusion = f32[12,12,1536]{2,1,0:T(8,128)S(1)} fusion(f32[12,12,1536]{2,1,0:T(8,128)S(1)} %all_to_all.77, f32[1536,1536]{1,0:T(8,128)} %all-gather.2.cloned.1.call-done), kind=kOutput, calls=%fused_computation.5 | convolution fusion | flops 4076863488 | bytes 11206656 | tf_op jit(solution)/shard_map/fxb,ab->fxa/dot_general | solution.py:63
  453.2 8.7 %copy.106 = f32[12,12,1536]{1,0,2:T(8,128)} copy(f32[12,12,1536]{2,1,0:T(8,128)S(1)} %fusion) | data formatting | bytes 1769472 | tf_op jit(solution)/shard_map/fxb,ab->fxa/dot_general | solution.py:63
  462.0 10.0 %reshape.747 = f32[32,1,6912]{2,1,0:T(1,128)} reshape(f32[1536,12,12]{2,1,0:T(8,128)} %bitcast.179) | data formatting | bytes 1769472
  472.0 8.5 %all-to-all-start.5 = ((f32[32,1,6912]{2,1,0:T(1,128)}), f32[32,1,6912]{2,1,0:T(1,128)S(1)}, u32[]{:S(2)}, u32[]{:S(2)}) async-start(f32[32,1,6912]{2,1,0:T(1,128)} %reshape.747), calls=%async_computation.5 | async-start | bytes 1769472 | tf_op jit(solution)/shard_map/all_to_all | solution.py:64
  480.9 21.0 %all-to-all-done.5 = f32[32,1,6912]{2,1,0:T(1,128)S(1)} async-done(((f32[32,1,6912]{2,1,0:T(1,128)}), f32[32,1,6912]{2,1,0:T(1,128)S(1)}, u32[]{:S(2)}, u32[]{:S(2)}) %all-to-all-start.5) | async-done | bytes 884768 | tf_op jit(solution)/shard_map/all_to_all | solution.py:64
  504.7 7.7 %reshape.748 = f32[1536,12,12]{2,1,0:T(8,128)} reshape(f32[32,6912]{1,0:T(8,128)S(1)} %reduce.4) | data formatting | bytes 1769472
  512.5 9.7 %copy.107 = f32[12,12,32,48]{3,1,2,0:T(8,128)S(1)} copy(f32[12,12,32,48]{1,0,3,2:T(8,128)} %bitcast.181) | data formatting | bytes 1769472 | tf_op jit(solution)/shard_map/all_to_all | solution.py:64
  529.4 5.7 copy.111
  544.9 12.1 %scatter_fusion = f32[2,13,256]{1,2,0:T(8,128)S(1)} fusion(f32[2,13,256]{1,2,0:T(8,128)S(1)} %broadcast_in_dim.15, s32[256]{0:T(256)S(1)} %bitcast.187, f32[256,13]{1,0:T(8,128)S(1)} %copy.116), kind=kCustom, calls=%fused_computation.4 | custom fusion | bytes 41984 | tf_op jit(solution)/shard_map/scatter | solution.py:105
  557.4 12.0 %all_to_all.94 = f32[8,1,832]{2,1,0:T(1,128)S(1)} all-to-all(f32[8,1,832]{2,1,0:T(1,128)S(1)} %reshape.749), channel_id=1, replica_groups=mesh['gx'=8,'gy'=32] {'gx'}, dimensions={0} | all-to-all | bytes 53248 | tf_op jit(solution)/shard_map/all_to_all | solution.py:109
  571.2 4.5 all-to-all-start.7
  576.7 7.8 %all-to-all-done.7 = f32[32,1,208]{2,1,0:T(1,128)S(1)} async-done(((f32[32,1,208]{2,1,0:T(1,128)}), f32[32,1,208]{2,1,0:T(1,128)S(1)}, u32[]{:S(2)}, u32[]{:S(2)}) %all-to-all-start.7) | async-done | bytes 26656 | tf_op jit(solution)/shard_map/all_to_all | solution.py:108
  (119 shorter events, 67.7 us)
Async XLA Ops:
  7.2 199.1 %all-gather.2.cloned.1.call-start = ((), (), s32[]{:S(2)}) async-start(), calls=%async_computation.8 | async-start | bytes 10616832 | tf_op jit(solution)/shard_map/all_gather | solution.py:51
  12.5 8.1 %copy-start.10 = (s32[48,384]{1,0:T(8,128)S(1)}, s32[48,384]{1,0:T(8,128)}, u32[]{:S(2)}) copy-start(s32[48,384]{1,0:T(8,128)} %param.16) | copy-start | bytes 221188
  12.5 125.8 %all-to-all-start = ((f32[8,12,48,384]{3,2,1,0:T(8,128)}), f32[8,12,48,384]{3,2,1,0:T(8,128)}, u32[]{:S(2)}, u32[]{:S(2)}) async-start(f32[8,12,48,384]{3,2,1,0:T(8,128)} %stack.14), calls=%async_computation | async-start | bytes 14155776 | tf_op jit(solution)/shard_map/all_to_all | solution.py:56
  20.6 121.7 %copy-start.6 = (f32[384,48]{0,1:T(8,128)}, f32[384,48]{0,1:T(8,128)S(1)}, u32[]{:S(2)}) copy-start(f32[384,48]{0,1:T(8,128)S(1)} %get-tuple-element.41) | copy-start | bytes 221188
  226.9 19.4 %copy-start = (f32[5,48,384]{2,1,0:T(8,128)S(1)}, f32[5,48,384]{2,1,0:T(8,128)}, u32[]{:S(2)}) copy-start(f32[5,48,384]{2,1,0:T(8,128)} %param.14) | copy-start | bytes 1105924
  237.0 29.9 %all-to-all-start.2 = ((f32[32,1,6912]{2,1,0:T(1,128)}), f32[32,1,6912]{2,1,0:T(1,128)S(1)}, u32[]{:S(2)}, u32[]{:S(2)}) async-start(f32[32,1,6912]{2,1,0:T(1,128)} %reshape.743), calls=%async_computation.2 | async-start | bytes 1769472 | tf_op jit(solution)/shard_map/all_to_all | solution.py:64
  247.0 2.7 copy-start.2
  247.7 0.6 copy-start.1
  294.5 89.6 %slice-start = ((s8[4718592]{0:T(1024)(128)(4,1)}), s8[4194304]{0:T(1024)(128)(4,1)S(1)}, s32[]{:S(2)}) async-start(s8[4718592]{0:T(1024)(128)(4,1)} %bitcast.185), calls=%async_computation.9 | async-start | bytes 8388608
  383.1 1.0 slice-start.1
  383.1 1.0 copy-start.7
  396.6 11.2 %copy-start.11 = (s32[256,1]{0,1:T(1,128)S(1)}, s32[256,1]{0,1:T(1,128)}, u32[]{:S(2)}) copy-start(s32[256,1]{0,1:T(1,128)} %param.20) | copy-start | bytes 3076
  402.3 26.3 %all-to-all-start.4 = ((f32[32,1,6912]{2,1,0:T(1,128)}), f32[32,1,6912]{2,1,0:T(1,128)S(1)}, u32[]{:S(2)}, u32[]{:S(2)}) async-start(f32[32,1,6912]{2,1,0:T(1,128)} %reshape.745), calls=%async_computation.4 | async-start | bytes 1769472 | tf_op jit(solution)/shard_map/all_to_all | solution.py:62
  408.2 20.4 %copy-start.3 = (s32[256,2,128]{0,1,2:T(2,128)}, s32[256,2,128]{0,1,2:T(2,128)S(1)}, u32[]{:S(2)}) copy-start(s32[256,2,128]{0,1,2:T(2,128)S(1)} %fusion.23) | copy-start | bytes 786436
  408.2 29.9 %copy-start.12 = (s32[256,3]{0,1:T(4,128)}, s32[256,3]{0,1:T(4,128)S(1)}, u32[]{:S(2)}) copy-start(s32[256,3]{0,1:T(4,128)S(1)} %reduce-window.9) | copy-start | bytes 9220
  461.9 18.5 %slice-start.2 = ((s32[256,3]{0,1:T(4,128)}), s32[256,2]{0,1:T(2,128)S(1)}, s32[]{:S(2)}) async-start(s32[256,3]{0,1:T(4,128)} %copy-done.12), calls=%async_computation.11 | async-start | bytes 4096 | tf_op jit(solution)/shard_map/slice.1
  461.9 18.5 %copy-start.4 = (s32[256,2,128]{0,1,2:T(2,128)S(1)}, s32[256,2,128]{0,1,2:T(2,128)}, u32[]{:S(2)}) copy-start(s32[256,2,128]{0,1,2:T(2,128)} %copy-done.3) | copy-start | bytes 786436
  462.0 18.8 %copy-start.15 = (f32[2,6]{1,0:T(2,128)S(1)}, f32[2,6]{1,0:T(2,128)}, u32[]{:S(2)}) copy-start(f32[2,6]{1,0:T(2,128)} %param.19) | copy-start | bytes 148
  462.0 18.8 %copy-start.13 = (s32[256]{0:T(256)S(1)}, s32[256]{0:T(256)}, u32[]{:S(2)}) copy-start(s32[256]{0:T(256)} %param.21) | copy-start | bytes 3076
  462.0 18.9 %copy-start.14 = (f32[2,256]{1,0:T(2,128)S(1)}, f32[2,256]{1,0:T(2,128)}, u32[]{:S(2)}) copy-start(f32[2,256]{1,0:T(2,128)} %param.22) | copy-start | bytes 6148
  472.0 30.0 %all-to-all-start.5 = ((f32[32,1,6912]{2,1,0:T(1,128)}), f32[32,1,6912]{2,1,0:T(1,128)S(1)}, u32[]{:S(2)}, u32[]{:S(2)}) async-start(f32[32,1,6912]{2,1,0:T(1,128)} %reshape.747), calls=%async_computation.5 | async-start | bytes 1769472 | tf_op jit(solution)/shard_map/all_to_all | solution.py:64
  526.5 2.6 copy-start.5
  526.5 2.6 copy-start.8
  529.3 5.7 copy-start.9
  571.2 13.3 %all-to-all-start.7 = ((f32[32,1,208]{2,1,0:T(1,128)}), f32[32,1,208]{2,1,0:T(1,128)S(1)}, u32[]{:S(2)}, u32[]{:S(2)}) async-start(f32[32,1,208]{2,1,0:T(1,128)} %reshape.751), calls=%async_computation.7 | async-start | bytes 65536 | tf_op jit(solution)/shard_map/all_to_all | solution.py:108
Sparse Core Ops, SparseCore 0:
  9.8 110.8 all-gather.1
